TPU v7x, 32 devices: a whole 2x2x4 slice. The times are simulated.
32 devices in a mesh: row: 8 (over y, x, core), col: 4 (over z).
Axes of the slice: x: 2, y: 2, z: 4, core: 2. Of those that a mesh axis runs over, the one named last changes fastest.
Arguments:
- features: bfloat16 [65536, 256], P(('row', 'col')), may hold values from -6 to 6
- w_self: bfloat16 [256, 256], replicated, may hold values from -0.375 to 0.375
- w_neigh: bfloat16 [256, 256], replicated, may hold values from -1.5 to 1.5
- bias: float32 [256], replicated, may hold values from -3 to 3
- hub_ids: int32 [6], replicated, may hold values from 0 to 7
- hub_adj: bfloat16 [32, 6, 2048, 256], P(('row', 'col')), may hold values from 0 to 2, as said below
- send_tile: int32 [32, 4, 2], P(('row', 'col')), may hold values from 0 to 15
- recv_count: int32 [32, 4], P(('row', 'col')), may hold values from 0 to 2, as said below
- recv_dst: int32 [32, 4, 2], P(('row', 'col')), may hold values from 0 to 15
- recv_adj: bfloat16 [32, 4, 2, 128, 128], P(('row', 'col')), may hold values from 0 to 2, as said below
- cotangent: bfloat16 [65536, 256], P(('row', 'col')), may hold values from -6 to 6
Outputs:
- output: bfloat16 [65536, 256], P(('row', 'col'))
- feature_grad: bfloat16 [65536, 256], P(('row', 'col'))
Inputs may be any that keep to these rules, and one draw needn't show every extreme that they name: `recv_count`: every device uses all 2 slots from at least one device of its row group. `hub_adj`: nonnegative edge weights. `recv_adj`: nonnegative edge weights.
All inputs are finite; a program needn't handle non-finite values.
Results may differ from a plain program's by a relative error of at most 0.0055.
Values may be sent and summed in bfloat16 or wider, within the bound.
No kernel may reach another device: no remote copies, remote signals or barrier semaphores. Data moves between devices by JAX's collectives and lax.ppermute only.
A program may use at most 64 MiB of HBM per device.

v0:
```python
import jax
import jax.numpy as jnp
from jax import lax
from jax.sharding import PartitionSpec as P


def shards(
    features,
    w_self,
    w_neigh,
    bias,
    hub_ids,
    hub_adj,
    send_tile,
    recv_count,
    recv_dst,
    recv_adj,
    cotangent,
):
    f32 = jnp.float32
    bf16 = jnp.bfloat16
    nodes, width = features.shape
    sections = hub_ids.shape[0]
    hub_rows = hub_adj.shape[3]
    peers, slots, tile = (recv_adj.shape[1], recv_adj.shape[2], recv_adj.shape[3])
    total = peers * slots
    count_tiles = nodes // tile
    row_pos = lax.axis_index("row")
    adjacency = hub_adj[0]
    own_hub = features[:hub_rows]
    every_hub = lax.all_gather(own_hub, "row", axis=0, tiled=True)
    hub_sum = jnp.zeros((nodes, width), f32)
    for section in range(sections):
        owner = hub_ids[section]
        block = lax.dynamic_slice_in_dim(every_hub, owner * hub_rows, hub_rows, 0)
        hub_sum = hub_sum + jnp.dot(adjacency[section], block, preferred_element_type=f32)
    offered = send_tile[0].reshape(total)
    outgoing = features.reshape(count_tiles, tile, width)[offered].reshape(
        peers, slots, tile, width
    )
    incoming = lax.all_to_all(outgoing, "col", split_axis=0, concat_axis=0, tiled=True)
    live = (
        (jnp.arange(slots, dtype=jnp.int32)[None, :] < recv_count[0][:, None])
        .astype(f32)
        .reshape(total)
    )
    landing = recv_dst[0].reshape(total)
    select = (landing[:, None] == jnp.arange(count_tiles, dtype=jnp.int32)[None, :]).astype(
        f32
    ) * live[:, None]
    weights = recv_adj[0].reshape(total, tile, tile)
    contrib = jnp.einsum(
        "sij,sjd->sid", weights, incoming.reshape(total, tile, width), preferred_element_type=f32
    )
    tile_sum = jnp.einsum("sn,sid->nid", select, contrib, precision=lax.Precision.HIGHEST).reshape(
        nodes, width
    )
    row_weight = jnp.sum(weights.astype(f32), axis=2)
    tile_deg = jnp.einsum("sn,si->ni", select, row_weight, precision=lax.Precision.HIGHEST).reshape(
        nodes
    )
    degree = 1.0 + jnp.sum(adjacency.astype(f32), axis=(0, 2)) + tile_deg
    agg = ((tile_sum + hub_sum) / degree[:, None]).astype(bf16)
    pre = (
        jnp.dot(features, w_self, preferred_element_type=f32)
        + jnp.dot(agg, w_neigh, preferred_element_type=f32)
        + bias
    )
    sig = jax.nn.sigmoid(pre)
    output = (pre * sig).astype(bf16)
    grad = (cotangent.astype(f32) * sig * (1.0 + pre * (1.0 - sig))).astype(bf16)
    contract = (((1,), (1,)), ((), ()))
    self_grad = lax.dot_general(grad, w_self, contract, preferred_element_type=f32)
    agg_grad = (
        lax.dot_general(grad, w_neigh, contract, preferred_element_type=f32) / degree[:, None]
    ).astype(bf16)
    hub_back = jnp.zeros((hub_rows, width), f32)
    for section in range(sections):
        partial_grad = lax.dot_general(
            adjacency[section], agg_grad, (((0,), (0,)), ((), ())), preferred_element_type=f32
        )
        summed_section = lax.psum(partial_grad, "row")
        hub_back = hub_back + jnp.where(row_pos == hub_ids[section], summed_section, 0.0)
    dest_rows = agg_grad.reshape(count_tiles, tile, width)[landing]
    slot_grad = (
        jnp.einsum("sij,sid->sjd", weights, dest_rows, preferred_element_type=f32)
        * live[:, None, None]
    ).astype(bf16)
    returned = lax.all_to_all(
        slot_grad.reshape(peers, slots, tile, width), "col", split_axis=0, concat_axis=0, tiled=True
    )
    owned = (offered[:, None] == jnp.arange(count_tiles, dtype=jnp.int32)[None, :]).astype(f32)
    tile_back = jnp.einsum(
        "sn,sid->nid",
        owned,
        returned.reshape(total, tile, width).astype(f32),
        precision=lax.Precision.HIGHEST,
    ).reshape(nodes, width)
    hub_padded = jnp.concatenate([hub_back, jnp.zeros((nodes - hub_rows, width), f32)], axis=0)
    feature_grad = (self_grad + tile_back + hub_padded).astype(bf16)
    return (output, feature_grad)


def solution(mesh):
    placed = (
        P(("row", "col"), None),
        P(),
        P(),
        P(),
        P(),
        P(("row", "col"), None, None, None),
        P(("row", "col"), None, None),
        P(("row", "col"), None),
        P(("row", "col"), None, None),
        P(("row", "col"), None, None, None, None),
        P(("row", "col"), None),
    )
    return jax.shard_map(
        shards,
        mesh=mesh,
        in_specs=placed,
        out_specs=(P(("row", "col"), None), P(("row", "col"), None)),
        check_vma=False,
    )
```

profile of v0, /device:TPU:0, one launch (start us, length us, event | category | flops | bytes accessed | tf_op | source)
XLA Modules:
  0.0 147.0 jit_solution(16033478632111042276)
XLA Ops:
  7.2 0.0 all-gather.2.cloned.1.call-start
  7.2 1.6 %slice.57 = bf16[256,256]{1,0:T(8,128)(2,1)} slice(bf16[2048,256]{1,0:T(8,128)(2,1)} %param.11), slice={[0:256], [0:256]} | slice | bytes 262144 | tf_op jit(solution)/shard_map/slice | solution.py:30
  8.8 0.0 all-gather.2.cloned.1.call-update
  8.8 0.8 copy.25
  9.6 0.1 reshape_squeeze.11
  9.7 0.8 copy.26
  10.4 0.1 reshape_squeeze.9
  10.6 2.6 %gather_fusion = bf16[8,128,256]{2,1,0:T(8,128)(2,1)} fusion(bf16[16,128,256]{2,1,0:T(8,128)(2,1)} %bitcast.113, s32[1024]{0:T(1024)S(1)} %pad_clamp_fusion.1), kind=kCustom, calls=%fused_computation | custom fusion | bytes 1048608 | tf_op jit(solution)/shard_map/gather | solution.py:38
  13.1 6.3 %all-to-all-start = ((bf16[4,2,128,256]{3,2,1,0:T(8,128)(2,1)}), bf16[4,2,128,256]{3,2,1,0:T(8,128)(2,1)S(1)}, u32[]{:S(2)}, u32[]{:S(2)}) async-start(bf16[4,2,128,256]{3,2,1,0:T(8,128)(2,1)} %bitcast.4), calls=%async_computation | async-start | bytes 1048576 | tf_op jit(solution)/shard_map/all_to_all | solution.py:41
  19.5 0.1 fusion.58
  19.6 3.9 %convert_reduce_fusion = f32[2048]{0:T(1024)S(1)} fusion(bf16[1,6,2048,256]{3,2,1,0:T(8,128)(2,1)} %param.16), kind=kLoop, calls=%fused_computation.2 | loop fusion | flops 6289408 | bytes 6299648 | tf_op jit(solution)/shard_map/reduce_sum | solution.py:62
  23.5 0.7 fusion.70
  27.9 0.1 eq.48
  28.0 0.1 reshape.153
  28.1 0.1 convert_reduce_fusion.1
  28.2 0.9 fusion.9
  29.1 1.8 %fusion.75 = f32[2048,256]{1,0:T(8,128)} fusion(bf16[2048,256]{1,0:T(8,128)(2,1)S(1)} %copy-done.1, bf16[256,256]{1,0:T(8,128)(2,1)S(1)} %copy-done.4), kind=kOutput, calls=%fused_computation.98 | convolution fusion | flops 268435456 | bytes 3276800 | tf_op jit(solution)/shard_map/dot_general | solution.py:65
  30.9 3.1 %all-to-all-done = bf16[4,2,128,256]{3,2,1,0:T(8,128)(2,1)S(1)} async-done(((bf16[4,2,128,256]{3,2,1,0:T(8,128)(2,1)}), bf16[4,2,128,256]{3,2,1,0:T(8,128)(2,1)S(1)}, u32[]{:S(2)}, u32[]{:S(2)}) %all-to-all-start) | async-done | bytes 524320 | tf_op jit(solution)/shard_map/all_to_all | solution.py:41
  34.0 0.3 fusion.76
  34.3 0.5 copy.39
  34.8 1.9 %fusion.24 = f32[16,128,256]{2,0,1:T(8,128)S(1)} fusion(f32[8,256,128]{1,0,2:T(8,128)S(1)} %copy.39, f32[8]{0:T(128)S(1)} %reshape.153, s32[8]{0:T(128)S(1)} %eq.48), kind=kOutput, calls=%fused_computation.45 | convolution fusion | flops 50331904 | bytes 3145792 | tf_op jit(solution)/shard_map/sn,sid->nid/dot_general | solution.py:55
  36.7 2.5 %copy.27 = f32[16,128,256]{2,1,0:T(8,128)} copy(f32[16,128,256]{2,0,1:T(8,128)S(1)} %fusion.24) | data formatting | bytes 4194304 | tf_op jit(solution)/shard_map/sn,sid->nid/dot_general | solution.py:55
  39.3 1.7 %fusion.22 = f32[256,2048]{0,1:T(8,128)S(1)} fusion(bf16[1,6,2048,256]{3,2,1,0:T(8,128)(2,1)} %param.16, bf16[2048,256]{1,0:T(8,128)(2,1)} %all-gather.2.cloned.1.call-done, s32[]{:T(128)S(6)} %select_n.77), kind=kOutput, calls=%fused_computation.43 | convolution fusion | flops 268435456 | bytes 3276804 | tf_op jit(solution)/shard_map/dot_general | solution.py:36
  41.1 1.7 %convolution_add_fusion.4 = f32[256,2048]{0,1:T(8,128)S(1)} fusion(f32[256,2048]{0,1:T(8,128)S(1)} %fusion.22, bf16[1,6,2048,256]{3,2,1,0:T(8,128)(2,1)} %param.16, bf16[2048,256]{1,0:T(8,128)(2,1)S(1)} %copy-done.6, s32[]{:T(128)S(6)} %select_n.78), kind=kOutput, calls=%fused_computation.9 | convolution fusion | flops 268959744 | bytes 5373956 | tf_op jit(solution)/shard_map/dot_general | solution.py:36
  42.7 1.7 %convolution_add_fusion.3 = f32[256,2048]{0,1:T(8,128)S(1)} fusion(f32[256,2048]{0,1:T(8,128)S(1)} %convolution_add_fusion.4, bf16[1,6,2048,256]{3,2,1,0:T(8,128)(2,1)} %param.16, bf16[2048,256]{1,0:T(8,128)(2,1)S(1)} %copy-done.6, s32[]{:T(128)S(6)} %select_n.79), kind=kOutput, calls=%fused_computation.8 | convolution fusion | flops 268959744 | bytes 5373956 | tf_op jit(solution)/shard_map/dot_general | solution.py:36
  44.4 1.7 %convolution_add_fusion.2 = f32[256,2048]{0,1:T(8,128)S(1)} fusion(f32[256,2048]{0,1:T(8,128)S(1)} %convolution_add_fusion.3, bf16[1,6,2048,256]{3,2,1,0:T(8,128)(2,1)} %param.16, bf16[2048,256]{1,0:T(8,128)(2,1)S(1)} %copy-done.6, s32[]{:T(128)S(6)} %select_n.80), kind=kOutput, calls=%fused_computation.7 | convolution fusion | flops 268959744 | bytes 5373956 | tf_op jit(solution)/shard_map/dot_general | solution.py:36
  46.1 3.1 %convolution_add_fusion.1 = f32[256,2048]{0,1:T(8,128)} fusion(f32[256,2048]{0,1:T(8,128)S(1)} %convolution_add_fusion.2, bf16[1,6,2048,256]{3,2,1,0:T(8,128)(2,1)} %param.16, bf16[2048,256]{1,0:T(8,128)(2,1)S(1)} %copy-done.6, s32[]{:T(128)S(6)} %select_n.81), kind=kOutput, calls=%fused_computation.6 | convolution fusion | flops 268959744 | bytes 5373956 | tf_op jit(solution)/shard_map/dot_general | solution.py:36
  49.3 5.3 %multiply_convert_fusion = (bf16[2048,256]{1,0:T(8,128)(2,1)S(1)}, bf16[2048,256]{1,0:T(8,128)(2,1)}) fusion(bf16[2048,256]{1,0:T(8,128)(2,1)} %param.21, f32[256]{0:T(256)S(1)} %copy-done.9, f32[2048,256]{1,0:T(8,128)S(1)} %copy-done.3, bf16[256,256]{1,0:T(8,128)(2,1)S(1)} %copy-done, f32[2048,256]{1,0:T(8,128)} %bitcast.117, ...), kind=kOutput, calls=%fused_computation.19 | convolution fusion | flops 546308096 | bytes 10757124 | tf_op jit(solution)/shard_map/dot_general | solution.py:66
  54.6 1.2 fusion.5
  55.8 2.5 %convolution_bitcast_fusion = f32[256,256]{1,0:T(8,128)} fusion(bf16[2048,256]{1,0:T(8,128)(2,1)S(1)} %fusion.5, bf16[1,6,2048,256]{3,2,1,0:T(8,128)(2,1)} %param.16), kind=kOutput, calls=%fused_computation.24 | convolution fusion | flops 268435456 | bytes 2359296 | tf_op jit(solution)/shard_map/dot_general | solution.py:79
  58.2 2.5 %convolution_bitcast_fusion.1 = f32[256,256]{1,0:T(8,128)} fusion(bf16[2048,256]{1,0:T(8,128)(2,1)S(1)} %fusion.5, bf16[1,6,2048,256]{3,2,1,0:T(8,128)(2,1)} %param.16), kind=kOutput, calls=%fused_computation.25 | convolution fusion | flops 268435456 | bytes 2359296 | tf_op jit(solution)/shard_map/dot_general | solution.py:79
  60.7 2.5 %convolution_bitcast_fusion.2 = f32[256,256]{1,0:T(8,128)} fusion(bf16[2048,256]{1,0:T(8,128)(2,1)S(1)} %fusion.5, bf16[1,6,2048,256]{3,2,1,0:T(8,128)(2,1)} %param.16), kind=kOutput, calls=%fused_computation.26 | convolution fusion | flops 268435456 | bytes 2359296 | tf_op jit(solution)/shard_map/dot_general | solution.py:79
  63.2 2.5 %convolution_bitcast_fusion.3 = f32[256,256]{1,0:T(8,128)} fusion(bf16[2048,256]{1,0:T(8,128)(2,1)S(1)} %fusion.5, bf16[1,6,2048,256]{3,2,1,0:T(8,128)(2,1)} %param.16), kind=kOutput, calls=%fused_computation.27 | convolution fusion | flops 268435456 | bytes 2359296 | tf_op jit(solution)/shard_map/dot_general | solution.py:79
  65.7 0.6 gather_fusion.1
  66.2 1.1 fusion.8
  67.4 3.5 %all-to-all-start.1 = ((bf16[4,2,128,256]{2,3,1,0:T(8,128)(2,1)}), bf16[4,2,128,256]{2,3,1,0:T(8,128)(2,1)S(1)}, u32[]{:S(2)}, u32[]{:S(2)}) async-start(bf16[4,2,128,256]{2,3,1,0:T(8,128)(2,1)} %bitcast.28), calls=%async_computation.1 | async-start | bytes 1048576 | tf_op jit(solution)/shard_map/all_to_all | solution.py:89
  70.9 0.2 all-reduce.4.cloned.1.call-start
  71.1 2.5 %convolution_bitcast_fusion.4 = f32[256,256]{1,0:T(8,128)} fusion(bf16[2048,256]{1,0:T(8,128)(2,1)S(1)} %fusion.5, bf16[1,6,2048,256]{3,2,1,0:T(8,128)(2,1)} %param.16), kind=kOutput, calls=%fused_computation.28 | convolution fusion | flops 268435456 | bytes 2359296 | tf_op jit(solution)/shard_map/dot_general | solution.py:79
  73.6 2.5 %convolution_bitcast_fusion.5 = f32[256,256]{1,0:T(8,128)} fusion(bf16[2048,256]{1,0:T(8,128)(2,1)S(1)} %fusion.5, bf16[1,6,2048,256]{3,2,1,0:T(8,128)(2,1)} %param.16), kind=kOutput, calls=%fused_computation.29 | convolution fusion | flops 268435456 | bytes 2359296 | tf_op jit(solution)/shard_map/dot_general | solution.py:79
  76.0 0.0 all-reduce.4.cloned.1.call-update
  79.8 0.1 eq.52
  79.9 5.0 %all-to-all-done.1 = bf16[4,2,128,256]{2,3,1,0:T(8,128)(2,1)S(1)} async-done(((bf16[4,2,128,256]{2,3,1,0:T(8,128)(2,1)}), bf16[4,2,128,256]{2,3,1,0:T(8,128)(2,1)S(1)}, u32[]{:S(2)}, u32[]{:S(2)}) %all-to-all-start.1) | async-done | bytes 524320 | tf_op jit(solution)/shard_map/all_to_all | solution.py:89
  84.9 0.4 copy.47
  85.3 0.5 fusion.49
  85.8 1.2 copy.32
  87.1 50.6 %all-reduce.4.cloned.1.call-done = (f32[256,256]{1,0:T(8,128)}, f32[256,256]{1,0:T(8,128)}, f32[256,256]{1,0:T(8,128)}, f32[256,256]{1,0:T(8,128)}, f32[256,256]{1,0:T(8,128)}, /*index=5*/f32[256,256]{1,0:T(8,128)}) async-done(((f32[256,256]{1,0:T(8,128)}, f32[256,256]{1,0:T(8,128)}, f32[256,256]{1,0:T(8,128)}, f32[256,256]{1,0:T(8,128)}, f32[256,256]{1,0:T(8,128)}, /*index=5*/f32[256,256]{1,0:T(8,128)}), ...) | async-done | bytes 1572880 | tf_op jit(solution)/shard_map/psum | solution.py:82
  137.6 1.1 select_add_fusion
  138.7 1.4 fusion.4
  (24 shorter events, 0.1 us)
Async XLA Ops:
  7.2 42.1 %copy-start = (bf16[256,256]{1,0:T(8,128)(2,1)S(1)}, bf16[256,256]{1,0:T(8,128)(2,1)}, u32[]{:S(2)}) copy-start(bf16[256,256]{1,0:T(8,128)(2,1)} %param.13) | copy-start | bytes 393220
  7.2 12.3 %copy-start.8 = (s32[1,4]{1,0:T(1,128)S(1)}, s32[1,4]{1,0:T(1,128)}, u32[]{:S(2)}) copy-start(s32[1,4]{1,0:T(1,128)} %param.18) | copy-start | bytes 52
  7.2 32.1 %all-gather.2.cloned.1.call-start = ((), (), s32[]{:S(2)}) async-start(), calls=%async_computation.2 | async-start | bytes 1179648 | tf_op jit(solution)/shard_map/all_gather | solution.py:31
  13.1 20.8 %all-to-all-start = ((bf16[4,2,128,256]{3,2,1,0:T(8,128)(2,1)}), bf16[4,2,128,256]{3,2,1,0:T(8,128)(2,1)S(1)}, u32[]{:S(2)}, u32[]{:S(2)}) async-start(bf16[4,2,128,256]{3,2,1,0:T(8,128)(2,1)} %bitcast.4), calls=%async_computation | async-start | bytes 1048576 | tf_op jit(solution)/shard_map/all_to_all | solution.py:41
  19.6 3.9 %copy-start.7 = (s32[6]{0:T(128)S(1)}, s32[6]{0:T(128)}, u32[]{:S(2)}) copy-start(s32[6]{0:T(128)} %param.15) | copy-start | bytes 76
  19.6 8.5 %copy-start.2 = (bf16[1,4,2,128,128]{4,3,2,1,0:T(8,128)(2,1)S(1)}, bf16[1,4,2,128,128]{4,3,2,1,0:T(8,128)(2,1)}, u32[]{:S(2)}) copy-start(bf16[1,4,2,128,128]{4,3,2,1,0:T(8,128)(2,1)} %param.20) | copy-start | bytes 786436
  19.6 9.5 %copy-start.1 = (bf16[2048,256]{1,0:T(8,128)(2,1)S(1)}, bf16[2048,256]{1,0:T(8,128)(2,1)}, u32[]{:S(2)}) copy-start(bf16[2048,256]{1,0:T(8,128)(2,1)} %param.11) | copy-start | bytes 3145732
  19.6 9.5 %copy-start.4 = (bf16[256,256]{1,0:T(8,128)(2,1)S(1)}, bf16[256,256]{1,0:T(8,128)(2,1)}, u32[]{:S(2)}) copy-start(bf16[256,256]{1,0:T(8,128)(2,1)} %param.12) | copy-start | bytes 393220
  39.3 1.8 %copy-start.6 = (bf16[2048,256]{1,0:T(8,128)(2,1)S(1)}, bf16[2048,256]{1,0:T(8,128)(2,1)}, u32[]{:S(2)}) copy-start(bf16[2048,256]{1,0:T(8,128)(2,1)} %all-gather.2.cloned.1.call-done) | copy-start | bytes 3145732
  46.1 3.2 %copy-start.3 = (f32[2048,256]{1,0:T(8,128)S(1)}, f32[2048,256]{1,0:T(8,128)}, u32[]{:S(2)}) copy-start(f32[2048,256]{1,0:T(8,128)} %fusion.75) | copy-start | bytes 6291460
  46.1 3.2 %copy-start.9 = (f32[256]{0:T(256)S(1)}, f32[256]{0:T(256)}, u32[]{:S(2)}) copy-start(f32[256]{0:T(256)} %param.14) | copy-start | bytes 3076
  67.4 17.5 %all-to-all-start.1 = ((bf16[4,2,128,256]{2,3,1,0:T(8,128)(2,1)}), bf16[4,2,128,256]{2,3,1,0:T(8,128)(2,1)S(1)}, u32[]{:S(2)}, u32[]{:S(2)}) async-start(bf16[4,2,128,256]{2,3,1,0:T(8,128)(2,1)} %bitcast.28), calls=%async_computation.1 | async-start | bytes 1048576 | tf_op jit(solution)/shard_map/all_to_all | solution.py:89
  70.9 66.8 %all-reduce.4.cloned.1.call-start = ((), (), s32[]{:S(2)}) async-start(), calls=%async_computation.3 | async-start | bytes 3145728 | tf_op jit(solution)/shard_map/psum | solution.py:82
  85.8 52.9 %copy-start.5 = (bf16[256,256]{1,0:T(8,128)(2,1)S(1)}, bf16[256,256]{1,0:T(8,128)(2,1)}, u32[]{:S(2)}) copy-start(bf16[256,256]{1,0:T(8,128)(2,1)} %param.12) | copy-start | bytes 393220
Sparse Core Ops, SparseCore 0:
  10.5 26.0 all-gather.1
  76.2 61.3 all-reduce.3
where the time goes:
time: 148 us; the launch traced here: 147 us
  waiting for transfers between devices  58.7 us (40%)
  matrix products  39.3 us (27%)
  between operations  21.7 us (15%)
  local copies, waits for them, and re-layouts  12.1 us (8%)
  starting transfers between devices  10.1 us (7%)
  other arithmetic  5.17 us (3%)
    psum x1, waiting for transfers between devices, shards(): summed_section = lax.psum(partial_grad, 'row')  50.6 us
    dot_general x6, matrix products, shards(): lax.dot_general(adjacency[section], agg_grad, (((0,), (0,)), ((), ())), p...  14.8 us
    dot_general x5, matrix products, shards(): jnp.dot(adjacency[section], block, preferred_element_type=f32)  9.91 us
    all_to_all x1, starting transfers between devices, shards(): lax.all_to_all(outgoing, 'col', split_axis=0, concat_axis=0, tiled=True)  6.35 us
    dot_general x1, matrix products, shards(): jnp.dot(agg, w_neigh, preferred_element_type=f32)  5.32 us
    all_to_all x1, waiting for transfers between devices, shards(): lax.all_to_all(slot_grad.reshape(peers, slots, tile, width), 'col', split...  4.98 us
    reduce_sum x1, other arithmetic, shards(): degree = 1.0 + jnp.sum(adjacency.astype(f32), axis=(0, 2)) + tile_deg  3.87 us
    all_to_all x1, starting transfers between devices, shards(): lax.all_to_all(slot_grad.reshape(peers, slots, tile, width), 'col', split...  3.47 us
  transfers between devices with their start and end apart: 4, of which 3 were waited for; matrix products, arithmetic and copies ran while one was open for 17% of the time, Pallas kernels for 0%

commit v1 on v0

--- a/solution.py
+++ b/solution.py
@@ -79,7 +79,11 @@
         partial_grad = lax.dot_general(
             adjacency[section], agg_grad, (((0,), (0,)), ((), ())), preferred_element_type=f32
         )
-        summed_section = lax.psum(partial_grad, "row")
+        summed_section = partial_grad
+        for hop in (1, 2, 4):
+            summed_section = summed_section + lax.ppermute(
+                summed_section, "row", [(dev, dev ^ hop) for dev in range(8)]
+            )
         hub_back = hub_back + jnp.where(row_pos == hub_ids[section], summed_section, 0.0)
     dest_rows = agg_grad.reshape(count_tiles, tile, width)[landing]
     slot_grad = (

time: 148 us -> 130 us (0.88)
  waiting for transfers between devices: 58.7 us -> 19.2 us
  starting transfers between devices: 10.1 us -> 25.1 us
  other arithmetic: 5.17 us -> 16.3 us
  matrix products: 39.3 us -> 32.8 us
    psum x1 -> x0, waiting for transfers between devices: 50.6 us -> none  [shards(): summed_section = lax.psum(partial_grad, 'row')]
    ppermute x0 -> x18, waiting for transfers between devices: none -> 16.2 us  [shards(): lax.ppermute(summed_section, 'row', [(dev, dev ^ hop) for dev in range(8)])]
    ppermute x0 -> x18, starting transfers between devices: none -> 15.3 us  [shards(): lax.ppermute(summed_section, 'row', [(dev, dev ^ hop) for dev in range(8)])]
    add x0 -> x12, other arithmetic: none -> 10.7 us  [shards(): summed_section + lax.ppermute(summed_section, 'row', [(dev, dev ^ hop) fo...]
    dot_general x6, matrix products: 14.8 us -> 8.11 us  [shards(): lax.dot_general(adjacency[section], agg_grad, (((0,), (0,)), ((), ())), p...]
    all_to_all x1, waiting for transfers between devices: 4.98 us -> 0.01 us  [shards(): lax.all_to_all(slot_grad.reshape(peers, slots, tile, width), 'col', split...]
  transfers between devices with their start and end apart: 4 -> 21, of which waited for: 3 -> 7; matrix products, arithmetic and copies ran while one was open for 17% -> 26% of each run, Pallas kernels for 0% -> 0%
where the time goes in v1:
time: 130 us; the launch traced here: 129 us
  matrix products  32.8 us (25%)
  starting transfers between devices  25.1 us (19%)
  between operations  22.2 us (17%)
  waiting for transfers between devices  19.2 us (15%)
  other arithmetic  16.3 us (13%)
  local copies, waits for them, and re-layouts  13.4 us (10%)
    ppermute x18, waiting for transfers between devices, shards(): lax.ppermute(summed_section, 'row', [(dev, dev ^ hop) for dev in range(8)])  16.2 us
    ppermute x18, starting transfers between devices, shards(): lax.ppermute(summed_section, 'row', [(dev, dev ^ hop) for dev in range(8)])  15.3 us
    add x12, other arithmetic, shards(): summed_section + lax.ppermute(summed_section, 'row', [(dev, dev ^ hop) fo...  10.7 us
    dot_general x5, matrix products, shards(): jnp.dot(adjacency[section], block, preferred_element_type=f32)  9.9 us
    dot_general x6, matrix products, shards(): lax.dot_general(adjacency[section], agg_grad, (((0,), (0,)), ((), ())), p...  8.11 us
    all_to_all x1, starting transfers between devices, shards(): lax.all_to_all(outgoing, 'col', split_axis=0, concat_axis=0, tiled=True)  6.35 us
    dot_general x1, matrix products, shards(): jnp.dot(agg, w_neigh, preferred_element_type=f32)  5.31 us
    reduce_sum x1, other arithmetic, shards(): degree = 1.0 + jnp.sum(adjacency.astype(f32), axis=(0, 2)) + tile_deg  3.79 us
  transfers between devices with their start and end apart: 21, of which 7 were waited for; matrix products, arithmetic and copies ran while one was open for 26% of the time, Pallas kernels for 0%

profile of v1, /device:TPU:0, one launch (start us, length us, event | category | flops | bytes accessed | tf_op | source)
XLA Modules:
  0.0 129.0 jit_solution(10222813803376104184)
XLA Ops:
  7.2 1.6 %slice.57 = bf16[256,256]{1,0:T(8,128)(2,1)} slice(bf16[2048,256]{1,0:T(8,128)(2,1)} %param.11), slice={[0:256], [0:256]} | slice | bytes 262144 | tf_op jit(solution)/shard_map/slice | solution.py:30
  10.6 2.6 %gather_fusion = bf16[8,128,256]{2,1,0:T(8,128)(2,1)} fusion(bf16[16,128,256]{2,1,0:T(8,128)(2,1)} %bitcast.115, s32[1024]{0:T(1024)S(1)} %pad_clamp_fusion.1), kind=kCustom, calls=%fused_computation | custom fusion | bytes 1048608 | tf_op jit(solution)/shard_map/gather | solution.py:38
  13.1 6.3 %all-to-all-start = ((bf16[4,2,128,256]{3,2,1,0:T(8,128)(2,1)}), bf16[4,2,128,256]{3,2,1,0:T(8,128)(2,1)S(1)}, u32[]{:S(2)}, u32[]{:S(2)}) async-start(bf16[4,2,128,256]{3,2,1,0:T(8,128)(2,1)} %bitcast.4), calls=%async_computation | async-start | bytes 1048576 | tf_op jit(solution)/shard_map/all_to_all | solution.py:41
  24.2 3.8 %convert_reduce_fusion = f32[2048]{0:T(1024)S(1)} fusion(bf16[1,6,2048,256]{3,2,1,0:T(8,128)(2,1)} %param.16), kind=kLoop, calls=%fused_computation.2 | loop fusion | flops 6289408 | bytes 6299648 | tf_op jit(solution)/shard_map/reduce_sum | solution.py:62
  28.3 0.9 fusion.7
  29.2 1.8 %fusion.73 = f32[2048,256]{1,0:T(8,128)} fusion(bf16[2048,256]{1,0:T(8,128)(2,1)S(1)} %copy-done.1, bf16[256,256]{1,0:T(8,128)(2,1)S(1)} %copy-done.4), kind=kOutput, calls=%fused_computation.97 | convolution fusion | flops 268435456 | bytes 3276800 | tf_op jit(solution)/shard_map/dot_general | solution.py:65
  31.0 3.0 %all-to-all-done = bf16[4,2,128,256]{3,2,1,0:T(8,128)(2,1)S(1)} async-done(((bf16[4,2,128,256]{3,2,1,0:T(8,128)(2,1)}), bf16[4,2,128,256]{3,2,1,0:T(8,128)(2,1)S(1)}, u32[]{:S(2)}, u32[]{:S(2)}) %all-to-all-start) | async-done | bytes 524320 | tf_op jit(solution)/shard_map/all_to_all | solution.py:41
  34.8 1.9 %fusion.22 = f32[16,128,256]{2,0,1:T(8,128)S(1)} fusion(f32[8,256,128]{1,0,2:T(8,128)S(1)} %copy.39, f32[8]{0:T(128)S(1)} %reshape.153, s32[8]{0:T(128)S(1)} %eq.48), kind=kOutput, calls=%fused_computation.44 | convolution fusion | flops 50331904 | bytes 3145792 | tf_op jit(solution)/shard_map/sn,sid->nid/dot_general | solution.py:55
  36.7 2.6 %copy.27 = f32[16,128,256]{2,1,0:T(8,128)} copy(f32[16,128,256]{2,0,1:T(8,128)S(1)} %fusion.22) | data formatting | bytes 4194304 | tf_op jit(solution)/shard_map/sn,sid->nid/dot_general | solution.py:55
  39.3 1.7 %fusion.20 = f32[256,2048]{0,1:T(8,128)S(1)} fusion(bf16[1,6,2048,256]{3,2,1,0:T(8,128)(2,1)} %param.16, bf16[2048,256]{1,0:T(8,128)(2,1)} %all-gather.2.cloned.1.call-done, s32[]{:T(128)S(6)} %select_n.77), kind=kOutput, calls=%fused_computation.42 | convolution fusion | flops 268435456 | bytes 3276804 | tf_op jit(solution)/shard_map/dot_general | solution.py:36
  41.1 1.7 %convolution_add_fusion.4 = f32[256,2048]{0,1:T(8,128)S(1)} fusion(f32[256,2048]{0,1:T(8,128)S(1)} %fusion.20, bf16[1,6,2048,256]{3,2,1,0:T(8,128)(2,1)} %param.16, bf16[2048,256]{1,0:T(8,128)(2,1)S(1)} %copy-done.6, s32[]{:T(128)S(6)} %select_n.78), kind=kOutput, calls=%fused_computation.9 | convolution fusion | flops 268959744 | bytes 5373956 | tf_op jit(solution)/shard_map/dot_general | solution.py:36
  42.8 1.7 %convolution_add_fusion.3 = f32[256,2048]{0,1:T(8,128)S(1)} fusion(f32[256,2048]{0,1:T(8,128)S(1)} %convolution_add_fusion.4, bf16[1,6,2048,256]{3,2,1,0:T(8,128)(2,1)} %param.16, bf16[2048,256]{1,0:T(8,128)(2,1)S(1)} %copy-done.6, s32[]{:T(128)S(6)} %select_n.79), kind=kOutput, calls=%fused_computation.8 | convolution fusion | flops 268959744 | bytes 5373956 | tf_op jit(solution)/shard_map/dot_general | solution.py:36
  44.4 1.7 %convolution_add_fusion.2 = f32[256,2048]{0,1:T(8,128)S(1)} fusion(f32[256,2048]{0,1:T(8,128)S(1)} %convolution_add_fusion.3, bf16[1,6,2048,256]{3,2,1,0:T(8,128)(2,1)} %param.16, bf16[2048,256]{1,0:T(8,128)(2,1)S(1)} %copy-done.6, s32[]{:T(128)S(6)} %select_n.80), kind=kOutput, calls=%fused_computation.7 | convolution fusion | flops 268959744 | bytes 5373956 | tf_op jit(solution)/shard_map/dot_general | solution.py:36
  46.1 3.1 %convolution_add_fusion.1 = f32[256,2048]{0,1:T(8,128)} fusion(f32[256,2048]{0,1:T(8,128)S(1)} %convolution_add_fusion.2, bf16[1,6,2048,256]{3,2,1,0:T(8,128)(2,1)} %param.16, bf16[2048,256]{1,0:T(8,128)(2,1)S(1)} %copy-done.6, s32[]{:T(128)S(6)} %select_n.81), kind=kOutput, calls=%fused_computation.6 | convolution fusion | flops 268959744 | bytes 5373956 | tf_op jit(solution)/shard_map/dot_general | solution.py:36
  49.3 5.3 %multiply_convert_fusion = (bf16[2048,256]{1,0:T(8,128)(2,1)S(1)}, bf16[2048,256]{1,0:T(8,128)(2,1)}) fusion(bf16[2048,256]{1,0:T(8,128)(2,1)} %param.21, f32[256]{0:T(256)S(1)} %copy-done.11, f32[2048,256]{1,0:T(8,128)S(1)} %copy-done.3, bf16[256,256]{1,0:T(8,128)(2,1)S(1)} %copy-done, f32[2048,256]{1,0:T(8,128)} %bitcast.119, ...), kind=kOutput, calls=%fused_computation.18 | convolution fusion | flops 546308096 | bytes 10757124 | tf_op jit(solution)/shard_map/dot_general | solution.py:66
  54.6 1.3 %fusion.3 = bf16[2048,256]{1,0:T(8,128)(2,1)S(1)} fusion(bf16[2048,256]{1,0:T(8,128)(2,1)S(1)} %get-tuple-element.2, bf16[256,256]{1,0:T(8,128)(2,1)S(1)} %copy-done, f32[2048]{0:T(1024)} %fusion.7), kind=kOutput, calls=%fused_computation.14 | convolution fusion | flops 269484032 | bytes 2236416 | tf_op jit(solution)/shard_map/dot_general | solution.py:75
  56.0 2.2 %convolution_bitcast_fusion.5 = f32[256,256]{1,0:T(8,128)S(1)} fusion(bf16[2048,256]{1,0:T(8,128)(2,1)S(1)} %fusion.3, bf16[1,6,2048,256]{3,2,1,0:T(8,128)(2,1)} %param.16), kind=kOutput, calls=%fused_computation.28 | convolution fusion | flops 268435456 | bytes 2359296 | tf_op jit(solution)/shard_map/dot_general | solution.py:79
  58.1 1.8 %convolution_bitcast_fusion.4 = f32[256,256]{1,0:T(8,128)S(1)} fusion(bf16[2048,256]{1,0:T(8,128)(2,1)S(1)} %fusion.3, bf16[1,6,2048,256]{3,2,1,0:T(8,128)(2,1)} %param.16), kind=kOutput, calls=%fused_computation.27 | convolution fusion | flops 268435456 | bytes 2359296 | tf_op jit(solution)/shard_map/dot_general | solution.py:79
  59.9 1.8 %convolution_bitcast_fusion.3 = f32[256,256]{1,0:T(8,128)S(1)} fusion(bf16[2048,256]{1,0:T(8,128)(2,1)S(1)} %fusion.3, bf16[1,6,2048,256]{3,2,1,0:T(8,128)(2,1)} %param.16), kind=kOutput, calls=%fused_computation.26 | convolution fusion | flops 268435456 | bytes 2359296 | tf_op jit(solution)/shard_map/dot_general | solution.py:79
  63.9 1.4 %convolution_bitcast_fusion = f32[256,256]{1,0:T(8,128)} fusion(bf16[2048,256]{1,0:T(8,128)(2,1)S(1)} %fusion.3, bf16[1,6,2048,256]{3,2,1,0:T(8,128)(2,1)S(1)} %bitcast.113), kind=kOutput, calls=%fused_computation.23 | convolution fusion | flops 268435456 | bytes 2359296 | tf_op jit(solution)/shard_map/dot_general | solution.py:79
  65.8 1.6 %collective-permute-start.1 = (f32[256,256]{1,0:T(8,128)S(1)}, f32[256,256]{1,0:T(8,128)}, u32[]{:S(2)}, u32[]{:S(2)}) collective-permute-start(f32[256,256]{1,0:T(8,128)S(1)} %add.197), channel_id=1, source_target_pairs={{0,8},{4,12},{8,0},{12,4},{16,24},{20,28},{24,16},{28,20},{1,9},{5... | collective-permute-start | bytes 786440 | tf_op jit(solution)/shard_map/ppermute | solution.py:84
  68.1 1.8 %gather_fusion.1 = bf16[8,128,256]{2,1,0:T(8,128)(2,1)S(1)} fusion(bf16[16,128,256]{2,1,0:T(8,128)(2,1)} %bitcast.121, s32[1024]{0:T(1024)S(1)} %pad_clamp_fusion), kind=kCustom, calls=%fused_computation.1 | custom fusion | bytes 1048608 | tf_op jit(solution)/shard_map/gather | solution.py:88
  69.9 1.0 add.204
  70.9 1.5 %collective-permute-start.7 = (f32[256,256]{1,0:T(8,128)S(1)}, f32[256,256]{1,0:T(8,128)}, u32[]{:S(2)}, u32[]{:S(2)}) collective-permute-start(f32[256,256]{1,0:T(8,128)S(1)} %add.204), channel_id=1, source_target_pairs={{0,8},{4,12},{8,0},{12,4},{16,24},{20,28},{24,16},{28,20},{1,9},{5... | collective-permute-start | bytes 786440 | tf_op jit(solution)/shard_map/ppermute | solution.py:84
  72.4 1.0 add.208
  74.1 1.0 add.212
  75.1 1.5 %collective-permute-start.13 = (f32[256,256]{1,0:T(8,128)S(1)}, f32[256,256]{1,0:T(8,128)}, u32[]{:S(2)}, u32[]{:S(2)}) collective-permute-start(f32[256,256]{1,0:T(8,128)S(1)} %add.212), channel_id=1, source_target_pairs={{0,8},{4,12},{8,0},{12,4},{16,24},{20,28},{24,16},{28,20},{1,9},{5... | collective-permute-start | bytes 786440 | tf_op jit(solution)/shard_map/ppermute | solution.py:84
  76.5 1.1 add.216
  78.3 1.7 %add.198 = f32[256,256]{1,0:T(8,128)} add(f32[256,256]{1,0:T(8,128)S(1)} %add.197, f32[256,256]{1,0:T(8,128)} %collective-permute-done.1) | non-fusion elementwise | flops 65536 | bytes 786432 | tf_op jit(solution)/shard_map/add | solution.py:84
  80.8 1.5 %collective-permute-start.2 = (f32[256,256]{1,0:T(8,128)}, f32[256,256]{1,0:T(8,128)S(1)}, u32[]{:S(2)}, u32[]{:S(2)}) collective-permute-start(f32[256,256]{1,0:T(8,128)} %add.198), channel_id=1, source_target_pairs={{0,16},{4,20},{8,24},{12,28},{16,0},{20,4},{24,8},{28,12},{1,17},{... | collective-permute-start | bytes 786440 | tf_op jit(solution)/shard_map/ppermute | solution.py:84
  82.3 1.1 fusion.6
  83.4 3.5 %all-to-all-start.1 = ((bf16[4,2,128,256]{2,3,1,0:T(8,128)(2,1)}), bf16[4,2,128,256]{2,3,1,0:T(8,128)(2,1)S(1)}, u32[]{:S(2)}, u32[]{:S(2)}) async-start(bf16[4,2,128,256]{2,3,1,0:T(8,128)(2,1)} %bitcast.28), calls=%async_computation.1 | async-start | bytes 1048576 | tf_op jit(solution)/shard_map/all_to_all | solution.py:93
  86.9 1.0 add.201
  88.5 1.0 add.205
  89.5 2.5 %collective-permute-done.10 = f32[256,256]{1,0:T(8,128)} collective-permute-done((f32[256,256]{1,0:T(8,128)S(1)}, f32[256,256]{1,0:T(8,128)}, u32[]{:S(2)}, u32[]{:S(2)}) %collective-permute-start.10) | collective-permute-done | bytes 262176 | tf_op jit(solution)/shard_map/ppermute | solution.py:84
  92.0 1.5 %collective-permute-start.8 = (f32[256,256]{1,0:T(8,128)S(1)}, f32[256,256]{1,0:T(8,128)}, u32[]{:S(2)}, u32[]{:S(2)}) collective-permute-start(f32[256,256]{1,0:T(8,128)S(1)} %add.205), channel_id=1, source_target_pairs={{0,16},{4,20},{8,24},{12,28},{16,0},{20,4},{24,8},{28,12},{1,17},{... | collective-permute-start | bytes 786440 | tf_op jit(solution)/shard_map/ppermute | solution.py:84
  93.5 1.0 add.209
  94.5 3.1 %collective-permute-done.13 = f32[256,256]{1,0:T(8,128)} collective-permute-done((f32[256,256]{1,0:T(8,128)S(1)}, f32[256,256]{1,0:T(8,128)}, u32[]{:S(2)}, u32[]{:S(2)}) %collective-permute-start.13) | collective-permute-done | bytes 262176 | tf_op jit(solution)/shard_map/ppermute | solution.py:84
  97.6 1.5 %collective-permute-start.11 = (f32[256,256]{1,0:T(8,128)S(1)}, f32[256,256]{1,0:T(8,128)}, u32[]{:S(2)}, u32[]{:S(2)}) collective-permute-start(f32[256,256]{1,0:T(8,128)S(1)} %add.209), channel_id=1, source_target_pairs={{0,16},{4,20},{8,24},{12,28},{16,0},{20,4},{24,8},{28,12},{1,17},{... | collective-permute-start | bytes 786440 | tf_op jit(solution)/shard_map/ppermute | solution.py:84
  99.1 1.0 add.213
  100.1 2.2 %collective-permute-done.16 = f32[256,256]{1,0:T(8,128)} collective-permute-done((f32[256,256]{1,0:T(8,128)S(1)}, f32[256,256]{1,0:T(8,128)}, u32[]{:S(2)}, u32[]{:S(2)}) %collective-permute-start.16) | collective-permute-done | bytes 262176 | tf_op jit(solution)/shard_map/ppermute | solution.py:84
  102.4 1.5 %collective-permute-start.14 = (f32[256,256]{1,0:T(8,128)S(1)}, f32[256,256]{1,0:T(8,128)}, u32[]{:S(2)}, u32[]{:S(2)}) collective-permute-start(f32[256,256]{1,0:T(8,128)S(1)} %add.213), channel_id=1, source_target_pairs={{0,16},{4,20},{8,24},{12,28},{16,0},{20,4},{24,8},{28,12},{1,17},{... | collective-permute-start | bytes 786440 | tf_op jit(solution)/shard_map/ppermute | solution.py:84
  103.9 1.0 add.217
  109.4 3.3 %collective-permute-done.14 = f32[256,256]{1,0:T(8,128)} collective-permute-done((f32[256,256]{1,0:T(8,128)S(1)}, f32[256,256]{1,0:T(8,128)}, u32[]{:S(2)}, u32[]{:S(2)}) %collective-permute-start.14) | collective-permute-done | bytes 262176 | tf_op jit(solution)/shard_map/ppermute | solution.py:84
  112.7 4.2 %collective-permute-done.17 = f32[256,256]{1,0:T(8,128)} collective-permute-done((f32[256,256]{1,0:T(8,128)S(1)}, f32[256,256]{1,0:T(8,128)}, u32[]{:S(2)}, u32[]{:S(2)}) %collective-permute-start.17) | collective-permute-done | bytes 262176 | tf_op jit(solution)/shard_map/ppermute | solution.py:84
  116.9 1.6 %select_add_fusion = f32[256,256]{1,0:T(8,128)S(1)} fusion(f32[256,256]{1,0:T(8,128)S(1)} %add.217, f32[256,256]{1,0:T(8,128)} %collective-permute-done.17, f32[256,256]{1,0:T(8,128)S(1)} %add.213, f32[256,256]{1,0:T(8,128)} %collective-permute-done.14, f32[256,256]{1,0:T(8,128)S(1)} %add.209, f32[256,256]{1,0:T(8,128)} %collective-permute-done.11, ...), kind=kLoop, calls=%fused_computation.60 | loop fusion | flops 1114112 | bytes 3407878 | tf_op jit(solution)/shard_map/add | solution.py:87
  119.5 1.2 copy.32
  120.7 1.5 %add_convert_fusion = bf16[2048,256]{1,0:T(8,128)(2,1)} fusion(f32[256,256]{1,0:T(8,128)S(1)} %select_add_fusion, f32[2048,256]{1,0:T(8,128)S(1)} %bitcast.114, bf16[2048,256]{1,0:T(8,128)(2,1)S(1)} %get-tuple-element.2, bf16[256,256]{1,0:T(8,128)(2,1)S(1)} %copy-done.5), kind=kOutput, calls=%fused_computation.17 | convolution fusion | flops 270008320 | bytes 4587520 | tf_op jit(solution)/shard_map/dot_general | solution.py:73
  (78 shorter events, 11.5 us)
Async XLA Ops:
  7.2 42.1 %copy-start = (bf16[256,256]{1,0:T(8,128)(2,1)S(1)}, bf16[256,256]{1,0:T(8,128)(2,1)}, u32[]{:S(2)}) copy-start(bf16[256,256]{1,0:T(8,128)(2,1)} %param.13) | copy-start | bytes 393220
  7.2 12.3 %copy-start.9 = (s32[6]{0:T(128)S(1)}, s32[6]{0:T(128)}, u32[]{:S(2)}) copy-start(s32[6]{0:T(128)} %param.15) | copy-start | bytes 76
  7.2 32.1 %all-gather.2.cloned.1.call-start = ((), (), s32[]{:S(2)}) async-start(), calls=%async_computation.2 | async-start | bytes 1179648 | tf_op jit(solution)/shard_map/all_gather | solution.py:31
  13.1 20.8 %all-to-all-start = ((bf16[4,2,128,256]{3,2,1,0:T(8,128)(2,1)}), bf16[4,2,128,256]{3,2,1,0:T(8,128)(2,1)S(1)}, u32[]{:S(2)}, u32[]{:S(2)}) async-start(bf16[4,2,128,256]{3,2,1,0:T(8,128)(2,1)} %bitcast.4), calls=%async_computation | async-start | bytes 1048576 | tf_op jit(solution)/shard_map/all_to_all | solution.py:41
  24.1 3.8 %copy-start.10 = (s32[1,4]{1,0:T(1,128)S(1)}, s32[1,4]{1,0:T(1,128)}, u32[]{:S(2)}) copy-start(s32[1,4]{1,0:T(1,128)} %param.18) | copy-start | bytes 52
  24.1 4.0 %copy-start.2 = (bf16[1,4,2,128,128]{4,3,2,1,0:T(8,128)(2,1)S(1)}, bf16[1,4,2,128,128]{4,3,2,1,0:T(8,128)(2,1)}, u32[]{:S(2)}) copy-start(bf16[1,4,2,128,128]{4,3,2,1,0:T(8,128)(2,1)} %param.20) | copy-start | bytes 786436
  24.1 5.0 %copy-start.1 = (bf16[2048,256]{1,0:T(8,128)(2,1)S(1)}, bf16[2048,256]{1,0:T(8,128)(2,1)}, u32[]{:S(2)}) copy-start(bf16[2048,256]{1,0:T(8,128)(2,1)} %param.11) | copy-start | bytes 3145732
  24.1 5.0 %copy-start.4 = (bf16[256,256]{1,0:T(8,128)(2,1)S(1)}, bf16[256,256]{1,0:T(8,128)(2,1)}, u32[]{:S(2)}) copy-start(bf16[256,256]{1,0:T(8,128)(2,1)} %param.12) | copy-start | bytes 393220
  39.3 1.7 %copy-start.6 = (bf16[2048,256]{1,0:T(8,128)(2,1)S(1)}, bf16[2048,256]{1,0:T(8,128)(2,1)}, u32[]{:S(2)}) copy-start(bf16[2048,256]{1,0:T(8,128)(2,1)} %all-gather.2.cloned.1.call-done) | copy-start | bytes 3145732
  46.1 3.2 %copy-start.3 = (f32[2048,256]{1,0:T(8,128)S(1)}, f32[2048,256]{1,0:T(8,128)}, u32[]{:S(2)}) copy-start(f32[2048,256]{1,0:T(8,128)} %fusion.73) | copy-start | bytes 6291460
  46.1 3.2 %copy-start.11 = (f32[256]{0:T(256)S(1)}, f32[256]{0:T(256)}, u32[]{:S(2)}) copy-start(f32[256]{0:T(256)} %param.14) | copy-start | bytes 3076
  54.6 7.1 %slice-start = ((s8[6291456]{0:T(1024)(128)(4,1)}), s8[2097152]{0:T(1024)(128)(4,1)S(1)}, s32[]{:S(2)}) async-start(s8[6291456]{0:T(1024)(128)(4,1)} %bitcast.112), calls=%async_computation.3 | async-start | bytes 4194304
  56.0 8.0 %copy-start.8 = (bf16[2048,256]{1,0:T(8,128)(2,1)}, bf16[2048,256]{1,0:T(8,128)(2,1)S(1)}, u32[]{:S(2)}) copy-start(bf16[2048,256]{1,0:T(8,128)(2,1)S(1)} %fusion.3) | copy-start | bytes 3145732
  56.0 5.7 %slice-start.1 = ((s8[6291456]{0:T(1024)(128)(4,1)}), s8[4194304]{0:T(1024)(128)(4,1)S(1)}, s32[]{:S(2)}) async-start(s8[6291456]{0:T(1024)(128)(4,1)} %bitcast.112), calls=%async_computation.4 | async-start | bytes 8388608
  62.8 2.6 %collective-permute-start = (f32[256,256]{1,0:T(8,128)S(1)}, f32[256,256]{1,0:T(8,128)S(1)}, u32[]{:S(2)}, u32[]{:S(2)}) collective-permute-start(f32[256,256]{1,0:T(8,128)S(1)} %convolution_bitcast_fusion.5), channel_id=1, source_target_pairs={{0,4},{4,0},{8,12},{12,8},{16,20},{20,16},{24,28},{28,24},{1,5},{5... | collective-permute-start | bytes 786440 | tf_op jit(solution)/shard_map/ppermute | solution.py:84
  62.8 3.0 %collective-permute-start.3 = (f32[256,256]{1,0:T(8,128)S(1)}, f32[256,256]{1,0:T(8,128)S(1)}, u32[]{:S(2)}, u32[]{:S(2)}) collective-permute-start(f32[256,256]{1,0:T(8,128)S(1)} %convolution_bitcast_fusion.4), channel_id=1, source_target_pairs={{0,4},{4,0},{8,12},{12,8},{16,20},{20,16},{24,28},{28,24},{1,5},{5... | collective-permute-start | bytes 786440 | tf_op jit(solution)/shard_map/ppermute | solution.py:84
  63.3 4.1 %collective-permute-start.6 = (f32[256,256]{1,0:T(8,128)S(1)}, f32[256,256]{1,0:T(8,128)S(1)}, u32[]{:S(2)}, u32[]{:S(2)}) collective-permute-start(f32[256,256]{1,0:T(8,128)S(1)} %convolution_bitcast_fusion.3), channel_id=1, source_target_pairs={{0,4},{4,0},{8,12},{12,8},{16,20},{20,16},{24,28},{28,24},{1,5},{5... | collective-permute-start | bytes 786440 | tf_op jit(solution)/shard_map/ppermute | solution.py:84
  63.4 7.5 %collective-permute-start.9 = (f32[256,256]{1,0:T(8,128)S(1)}, f32[256,256]{1,0:T(8,128)}, u32[]{:S(2)}, u32[]{:S(2)}) collective-permute-start(f32[256,256]{1,0:T(8,128)S(1)} %convolution_bitcast_fusion.2), channel_id=1, source_target_pairs={{0,4},{4,0},{8,12},{12,8},{16,20},{20,16},{24,28},{28,24},{1,5},{5... | collective-permute-start | bytes 786440 | tf_op jit(solution)/shard_map/ppermute | solution.py:84
  63.8 9.5 %collective-permute-start.12 = (f32[256,256]{1,0:T(8,128)S(1)}, f32[256,256]{1,0:T(8,128)}, u32[]{:S(2)}, u32[]{:S(2)}) collective-permute-start(f32[256,256]{1,0:T(8,128)S(1)} %convolution_bitcast_fusion.1), channel_id=1, source_target_pairs={{0,4},{4,0},{8,12},{12,8},{16,20},{20,16},{24,28},{28,24},{1,5},{5... | collective-permute-start | bytes 786440 | tf_op jit(solution)/shard_map/ppermute | solution.py:84
  65.3 9.7 %collective-permute-start.15 = (f32[256,256]{1,0:T(8,128)}, f32[256,256]{1,0:T(8,128)}, u32[]{:S(2)}, u32[]{:S(2)}) collective-permute-start(f32[256,256]{1,0:T(8,128)} %convolution_bitcast_fusion), channel_id=1, source_target_pairs={{0,4},{4,0},{8,12},{12,8},{16,20},{20,16},{24,28},{28,24},{1,5},{5... | collective-permute-start | bytes 786440 | tf_op jit(solution)/shard_map/ppermute | solution.py:84
  65.8 11.8 %collective-permute-start.1 = (f32[256,256]{1,0:T(8,128)S(1)}, f32[256,256]{1,0:T(8,128)}, u32[]{:S(2)}, u32[]{:S(2)}) collective-permute-start(f32[256,256]{1,0:T(8,128)S(1)} %add.197), channel_id=1, source_target_pairs={{0,8},{4,12},{8,0},{12,4},{16,24},{20,28},{24,16},{28,20},{1,9},{5... | collective-permute-start | bytes 786440 | tf_op jit(solution)/shard_map/ppermute | solution.py:84
  67.4 0.7 copy-start.7
  67.4 13.4 %collective-permute-start.4 = (f32[256,256]{1,0:T(8,128)S(1)}, f32[256,256]{1,0:T(8,128)}, u32[]{:S(2)}, u32[]{:S(2)}) collective-permute-start(f32[256,256]{1,0:T(8,128)S(1)} %add.200), channel_id=1, source_target_pairs={{0,8},{4,12},{8,0},{12,4},{16,24},{20,28},{24,16},{28,20},{1,9},{5... | collective-permute-start | bytes 786440 | tf_op jit(solution)/shard_map/ppermute | solution.py:84
  70.9 17.0 %collective-permute-start.7 = (f32[256,256]{1,0:T(8,128)S(1)}, f32[256,256]{1,0:T(8,128)}, u32[]{:S(2)}, u32[]{:S(2)}) collective-permute-start(f32[256,256]{1,0:T(8,128)S(1)} %add.204), channel_id=1, source_target_pairs={{0,8},{4,12},{8,0},{12,4},{16,24},{20,28},{24,16},{28,20},{1,9},{5... | collective-permute-start | bytes 786440 | tf_op jit(solution)/shard_map/ppermute | solution.py:84
  73.4 18.6 %collective-permute-start.10 = (f32[256,256]{1,0:T(8,128)S(1)}, f32[256,256]{1,0:T(8,128)}, u32[]{:S(2)}, u32[]{:S(2)}) collective-permute-start(f32[256,256]{1,0:T(8,128)S(1)} %add.208), channel_id=1, source_target_pairs={{0,8},{4,12},{8,0},{12,4},{16,24},{20,28},{24,16},{28,20},{1,9},{5... | collective-permute-start | bytes 786440 | tf_op jit(solution)/shard_map/ppermute | solution.py:84
  75.1 22.6 %collective-permute-start.13 = (f32[256,256]{1,0:T(8,128)S(1)}, f32[256,256]{1,0:T(8,128)}, u32[]{:S(2)}, u32[]{:S(2)}) collective-permute-start(f32[256,256]{1,0:T(8,128)S(1)} %add.212), channel_id=1, source_target_pairs={{0,8},{4,12},{8,0},{12,4},{16,24},{20,28},{24,16},{28,20},{1,9},{5... | collective-permute-start | bytes 786440 | tf_op jit(solution)/shard_map/ppermute | solution.py:84
  77.6 24.7 %collective-permute-start.16 = (f32[256,256]{1,0:T(8,128)S(1)}, f32[256,256]{1,0:T(8,128)}, u32[]{:S(2)}, u32[]{:S(2)}) collective-permute-start(f32[256,256]{1,0:T(8,128)S(1)} %add.216), channel_id=1, source_target_pairs={{0,8},{4,12},{8,0},{12,4},{16,24},{20,28},{24,16},{28,20},{1,9},{5... | collective-permute-start | bytes 786440 | tf_op jit(solution)/shard_map/ppermute | solution.py:84
  80.8 24.1 %collective-permute-start.2 = (f32[256,256]{1,0:T(8,128)}, f32[256,256]{1,0:T(8,128)S(1)}, u32[]{:S(2)}, u32[]{:S(2)}) collective-permute-start(f32[256,256]{1,0:T(8,128)} %add.198), channel_id=1, source_target_pairs={{0,16},{4,20},{8,24},{12,28},{16,0},{20,4},{24,8},{28,12},{1,17},{... | collective-permute-start | bytes 786440 | tf_op jit(solution)/shard_map/ppermute | solution.py:84
  83.4 35.0 %all-to-all-start.1 = ((bf16[4,2,128,256]{2,3,1,0:T(8,128)(2,1)}), bf16[4,2,128,256]{2,3,1,0:T(8,128)(2,1)S(1)}, u32[]{:S(2)}, u32[]{:S(2)}) async-start(bf16[4,2,128,256]{2,3,1,0:T(8,128)(2,1)} %bitcast.28), calls=%async_computation.1 | async-start | bytes 1048576 | tf_op jit(solution)/shard_map/all_to_all | solution.py:93
  87.9 21.5 %collective-permute-start.5 = (f32[256,256]{1,0:T(8,128)S(1)}, f32[256,256]{1,0:T(8,128)}, u32[]{:S(2)}, u32[]{:S(2)}) collective-permute-start(f32[256,256]{1,0:T(8,128)S(1)} %add.201), channel_id=1, source_target_pairs={{0,16},{4,20},{8,24},{12,28},{16,0},{20,4},{24,8},{28,12},{1,17},{... | collective-permute-start | bytes 786440 | tf_op jit(solution)/shard_map/ppermute | solution.py:84
  92.0 17.4 %collective-permute-start.8 = (f32[256,256]{1,0:T(8,128)S(1)}, f32[256,256]{1,0:T(8,128)}, u32[]{:S(2)}, u32[]{:S(2)}) collective-permute-start(f32[256,256]{1,0:T(8,128)S(1)} %add.205), channel_id=1, source_target_pairs={{0,16},{4,20},{8,24},{12,28},{16,0},{20,4},{24,8},{28,12},{1,17},{... | collective-permute-start | bytes 786440 | tf_op jit(solution)/shard_map/ppermute | solution.py:84
  97.6 11.8 %collective-permute-start.11 = (f32[256,256]{1,0:T(8,128)S(1)}, f32[256,256]{1,0:T(8,128)}, u32[]{:S(2)}, u32[]{:S(2)}) collective-permute-start(f32[256,256]{1,0:T(8,128)S(1)} %add.209), channel_id=1, source_target_pairs={{0,16},{4,20},{8,24},{12,28},{16,0},{20,4},{24,8},{28,12},{1,17},{... | collective-permute-start | bytes 786440 | tf_op jit(solution)/shard_map/ppermute | solution.py:84
  102.4 10.4 %collective-permute-start.14 = (f32[256,256]{1,0:T(8,128)S(1)}, f32[256,256]{1,0:T(8,128)}, u32[]{:S(2)}, u32[]{:S(2)}) collective-permute-start(f32[256,256]{1,0:T(8,128)S(1)} %add.213), channel_id=1, source_target_pairs={{0,16},{4,20},{8,24},{12,28},{16,0},{20,4},{24,8},{28,12},{1,17},{... | collective-permute-start | bytes 786440 | tf_op jit(solution)/shard_map/ppermute | solution.py:84
  104.9 12.1 %collective-permute-start.17 = (f32[256,256]{1,0:T(8,128)S(1)}, f32[256,256]{1,0:T(8,128)}, u32[]{:S(2)}, u32[]{:S(2)}) collective-permute-start(f32[256,256]{1,0:T(8,128)S(1)} %add.217), channel_id=1, source_target_pairs={{0,16},{4,20},{8,24},{12,28},{16,0},{20,4},{24,8},{28,12},{1,17},{... | collective-permute-start | bytes 786440 | tf_op jit(solution)/shard_map/ppermute | solution.py:84
  119.4 1.2 copy-start.5
Sparse Core Ops, SparseCore 0:
  10.5 26.0 all-gather.1
